TPU v7x, 32 devices: a whole 2x2x4 slice. The times are simulated.
32 devices in a mesh: energy: 8 (over y, x, core), space: 4 (over z).
Axes of the slice: x: 2, y: 2, z: 4, core: 2. Of those that a mesh axis runs over, the one named last changes fastest.
Arguments:
- green: bfloat16 [4, 8, 4, 384, 384], P(None, 'energy', 'space'), may hold values from -6 to 6
- v_diag: bfloat16 [4, 384, 384], P('space'), may hold values from -0.3125 to 0.3125
- v_low: bfloat16 [4, 384, 384], P('space'), may hold values from -0.3125 to 0.3125
- energy_slot: int32 [8], replicated, may hold values from 0 to 7, each once
Outputs:
- sigma: bfloat16 [2, 8, 4, 384, 384], P(None, None, 'space', 'energy')
Inputs may be any that keep to these rules, and one draw needn't show every extreme that they name: `energy_slot`: each grid energy appears in exactly one slot.
All inputs are finite; a program needn't handle non-finite values.
Results may differ from a plain program's by a relative error of at most 0.0066.
Values may be sent and summed in bfloat16 or wider, within the bound.
No kernel may reach another device: no remote copies, remote signals or barrier semaphores. Data moves between devices by JAX's collectives and lax.ppermute only.
A program may use at most 64 MiB of HBM per device.

v0:
```python
import math
import jax
import jax.numpy as jnp
from jax import lax
from jax.sharding import PartitionSpec as P


def shifted(value, axis, steps):
    count = lax.axis_size(axis)
    leading, last = (max(0, -steps), min(count, count - steps))
    return lax.ppermute(value, axis, [(source, source + steps) for source in range(leading, last)])


def apply_table(table, values):
    return jnp.dot(
        table, values, precision=lax.Precision.HIGHEST, preferred_element_type=jnp.float32
    )


def spectra(cos_table, sin_table, real_part, imag_part):
    out_real = apply_table(cos_table, real_part) + apply_table(sin_table, imag_part)
    out_imag = apply_table(cos_table, imag_part) - apply_table(sin_table, real_part)
    return (out_real, out_imag)


def to_slots(cos_table, sin_table, real_part, imag_part):
    factor = 1.0 / cos_table.shape[0]
    cos_back = cos_table.T
    sin_back = sin_table.T
    out_real = (apply_table(cos_back, real_part) - apply_table(sin_back, imag_part)) * factor
    out_imag = (apply_table(cos_back, imag_part) + apply_table(sin_back, real_part)) * factor
    return (out_real, out_imag)


def sandwich(matrix, polar):
    left = jnp.einsum("ij,cejk->ceik", matrix, polar, preferred_element_type=jnp.float32).astype(
        jnp.bfloat16
    )
    return jnp.einsum("ceij,kj->ceik", left, matrix, preferred_element_type=jnp.float32)


def sandwich_t(matrix, polar):
    left = jnp.einsum("ji,cejk->ceik", matrix, polar, preferred_element_type=jnp.float32).astype(
        jnp.bfloat16
    )
    return jnp.einsum("ceij,jk->ceik", left, matrix, preferred_element_type=jnp.float32)


def shards(green, v_diag, v_low, energy_slot):
    energies = energy_slot.shape[0]
    period = 2 * energies
    frequency = jnp.arange(period, dtype=jnp.int32)
    phases = frequency[:, None] * energy_slot[None, :] % period
    angles = phases.astype(jnp.float32) * (2.0 * math.pi / period)
    cos_table = jnp.cos(angles)
    sin_table = jnp.sin(angles)
    scaling = energies ** (-0.5)
    arrived = lax.all_to_all(green[:, :, 0], "energy", split_axis=2, concat_axis=1, tiled=True)
    row_count = arrived.shape[2]
    col_count = arrived.shape[3]
    flattened = arrived.reshape((4, energies, row_count * col_count)).astype(jnp.float32)
    lesser_re, lesser_im = spectra(cos_table, sin_table, flattened[0], flattened[1])
    greater_re, greater_im = spectra(cos_table, sin_table, flattened[2], flattened[3])
    cross_re = lesser_re * greater_re + lesser_im * greater_im
    cross_im = lesser_im * greater_re - lesser_re * greater_im
    corr_re, corr_im = to_slots(cos_table, sin_table, cross_re, cross_im)
    polar_slot = (
        jnp.stack([corr_im * scaling, -corr_re * scaling])
        .reshape((2, energies, row_count, col_count))
        .astype(jnp.bfloat16)
    )
    polar = lax.all_to_all(polar_slot, "energy", split_axis=1, concat_axis=2, tiled=True)
    diagonal = v_diag[0]
    lower = v_low[0]
    own_term = sandwich(diagonal, polar)
    below = shifted(polar, "space", 1)
    handed = sandwich_t(lower, polar).astype(jnp.bfloat16)
    received = shifted(handed, "space", -1)
    total = own_term + sandwich(lower, below) + received.astype(jnp.float32)
    screened = total.astype(jnp.bfloat16)
    screened_rows = lax.all_to_all(screened, "energy", split_axis=2, concat_axis=1, tiled=True)
    weights = screened_rows.reshape((2, energies, row_count * col_count)).astype(jnp.float32)
    weight_re, weight_im = spectra(cos_table, sin_table, weights[0], weights[1])
    joint_re = lesser_re * weight_re - lesser_im * weight_im
    joint_im = lesser_re * weight_im + lesser_im * weight_re
    conv_re, conv_im = to_slots(cos_table, sin_table, joint_re, joint_im)
    sigma = (
        jnp.stack([-conv_im * scaling, conv_re * scaling])
        .reshape((2, energies, row_count, col_count))
        .astype(jnp.bfloat16)
    )
    return sigma[:, :, None]


def solution(mesh):
    in_specs = (
        P(None, "energy", "space", None, None),
        P("space", None, None),
        P("space", None, None),
        P(),
    )
    out_specs = P(None, None, "space", "energy", None)
    return jax.shard_map(shards, mesh=mesh, in_specs=in_specs, out_specs=out_specs, check_vma=False)
```

profile of v0, /device:TPU:24, one launch (start us, length us, event | category | flops | bytes accessed | tf_op | source)
XLA Modules:
  0.0 103.2 jit_solution(476986298993754648)
XLA Ops:
  0.0 2.2 %copy.56 = bf16[4,1,1,384,384]{4,0,3,2,1:T(4,128)(2,1)S(1)} copy(bf16[4,1,1,384,384]{4,3,2,1,0:T(8,128)(2,1)} %param.4) | data formatting | bytes 2359296 | tf_op args[0]
  2.2 20.3 %all_to_all.30 = bf16[4,1,384,384]{3,0,1,2:T(4,128)(2,1)S(1)} all-to-all(bf16[4,1,384,384]{3,0,1,2:T(4,128)(2,1)S(1)} %bitcast.85), channel_id=1, replica_groups=mesh['energy'=8,'space'=4] {'energy'}, dimensions={2} | all-to-all | bytes 2359296 | tf_op jit(solution)/shard_map/all_to_all | solution.py:58
  22.5 7.5 %slice_reduce_fusion.3 = (bf16[384,384]{1,0:T(8,128)(2,1)S(1)}, bf16[384,384]{1,0:T(8,128)(2,1)S(1)}, bf16[384,384]{1,0:T(8,128)(2,1)S(1)}, bf16[384,384]{1,0:T(8,128)(2,1)S(1)}) fusion(bf16[4,1,384,384]{3,0,1,2:T(4,128)(2,1)S(1)} %all_to_all.30), kind=kLoop, calls=%fused_computation.42 | loop fusion | bytes 2359296 | tf_op jit(solution)/shard_map/slice | solution.py:63
  30.0 0.0 copy-start.3
  30.0 0.1 squeeze.30
  30.2 0.1 squeeze.31
  30.3 0.1 squeeze.29
  30.5 0.1 squeeze.28
  30.6 0.1 copy-done.3
  30.7 0.7 fusion.52
  31.4 0.7 fusion.50
  32.0 0.7 convolution_subtract_fusion.2
  32.7 0.7 fusion.46
  33.4 0.7 fusion.48
  34.0 0.7 convolution_subtract_fusion.1
  34.7 0.7 convolution_add_fusion.1
  35.4 2.1 %multiply_subtract_fusion.1 = (f32[16,18432]{1,0:T(8,128)S(1)}, f32[16,18432]{1,0:T(8,128)S(1)}, f32[16,18432]{1,0:T(8,128)}) fusion(f32[16,18432]{1,0:T(8,128)S(1)} %convolution_subtract_fusion.1, f32[16,18432]{1,0:T(8,128)S(1)} %convolution_subtract_fusion.2, f32[16,18432]{1,0:T(8,128)S(1)} %convolution_add_fusion.1, f32[16,18432]{1,0:T(8,128)S(1)} %fusion.52, ...), kind=kOutput, calls=%fused_computation.38 | convolution fusion | flops 30377728 | bytes 8552480 | tf_op jit(solution)/shard_map/dot_general | solution.py:15
  37.4 0.7 fusion.44
  38.2 0.7 fusion.42
  38.9 0.8 fusion.8
  39.7 0.8 fusion.9
  40.5 0.1 pad_maximum_fusion
  40.6 12.8 %all_to_all.31 = bf16[2,8,48,384]{3,2,0,1:T(8,128)(2,1)S(1)} all-to-all(bf16[2,8,48,384]{3,2,0,1:T(8,128)(2,1)S(1)} %pad_maximum_fusion), channel_id=1, replica_groups=mesh['energy'=8,'space'=4] {'energy'}, dimensions={1} | all-to-all | bytes 1179648 | tf_op jit(solution)/shard_map/all_to_all | solution.py:72
  53.4 0.1 copy.39
  53.5 1.1 %copy.43 = bf16[2,1,384,384]{2,3,0,1:T(8,128)(2,1)} copy(bf16[2,1,384,384]{3,2,0,1:T(8,128)(2,1)S(1)} %bitcast.82) | data formatting | bytes 1179648 | tf_op jit(solution)/shard_map/all_to_all | solution.py:72
  54.6 1.9 %fusion.17 = bf16[2,1,384,384]{3,2,0,1:T(8,128)(2,1)} fusion(bf16[2,384,384]{2,1,0:T(8,128)(2,1)S(1)} %bitcast.83, bf16[1,384,384]{2,1,0:T(8,128)(2,1)S(1)} %copy-done), kind=kOutput, calls=%fused_computation.32 | convolution fusion | flops 453574656 | bytes 1474560 | tf_op jit(solution)/shard_map/ceij,jk->ceik/dot_general | solution.py:46
  56.5 3.2 %collective-permute-start.1 = (bf16[2,1,384,384]{3,2,0,1:T(8,128)(2,1)}, bf16[2,1,384,384]{3,2,0,1:T(8,128)(2,1)}, u32[]{:S(2)}, u32[]{:S(2)}) collective-permute-start(bf16[2,1,384,384]{3,2,0,1:T(8,128)(2,1)} %fusion.17), channel_id=1, source_target_pairs={{1,0},{2,1},{3,2},{5,4},{6,5},{7,6},{9,8},{10,9},{11,10},{13,12},{... | collective-permute-start | bytes 1769480 | tf_op jit(solution)/shard_map/ppermute | solution.py:11
  59.7 1.5 %collective-permute-start = (bf16[2,1,384,384]{2,3,0,1:T(8,128)(2,1)}, bf16[2,1,384,384]{2,3,0,1:T(8,128)(2,1)}, u32[]{:S(2)}, u32[]{:S(2)}) collective-permute-start(bf16[2,1,384,384]{2,3,0,1:T(8,128)(2,1)} %copy.43), channel_id=1, source_target_pairs={{0,1},{1,2},{2,3},{4,5},{5,6},{6,7},{8,9},{9,10},{10,11},{12,13},{... | collective-permute-start | bytes 1769480 | tf_op jit(solution)/shard_map/ppermute | solution.py:11
  61.2 0.0 copy-done.2
  61.2 1.1 %fusion.14 = f32[2,384,384]{2,1,0:T(8,128)S(1)} fusion(bf16[2,384,384]{2,1,0:T(8,128)(2,1)S(1)} %bitcast.84, bf16[1,384,384]{2,1,0:T(8,128)(2,1)S(1)} %copy-done.2), kind=kOutput, calls=%fused_computation.29 | convolution fusion | flops 453279744 | bytes 2064384 | tf_op jit(solution)/shard_map/ceij,kj->ceik/dot_general | solution.py:39
  62.3 9.4 %collective-permute-done.1 = bf16[2,1,384,384]{3,2,0,1:T(8,128)(2,1)} collective-permute-done((bf16[2,1,384,384]{3,2,0,1:T(8,128)(2,1)}, bf16[2,1,384,384]{3,2,0,1:T(8,128)(2,1)}, u32[]{:S(2)}, u32[]{:S(2)}) %collective-permute-start.1) | collective-permute-done | bytes 589856 | tf_op jit(solution)/shard_map/ppermute | solution.py:11
  71.6 5.0 %collective-permute-done = bf16[2,1,384,384]{2,3,0,1:T(8,128)(2,1)} collective-permute-done((bf16[2,1,384,384]{2,3,0,1:T(8,128)(2,1)}, bf16[2,1,384,384]{2,3,0,1:T(8,128)(2,1)}, u32[]{:S(2)}, u32[]{:S(2)}) %collective-permute-start) | collective-permute-done | bytes 589856 | tf_op jit(solution)/shard_map/ppermute | solution.py:11
  76.6 2.3 %add_convert_fusion = bf16[2,1,384,384]{3,2,0,1:T(8,128)(2,1)S(1)} fusion(bf16[2,1,384,384]{3,2,0,1:T(8,128)(2,1)} %collective-permute-done.1, f32[2,384,384]{2,1,0:T(8,128)S(1)} %fusion.14, bf16[2,1,384,384]{2,3,0,1:T(8,128)(2,1)} %collective-permute-done, bf16[1,384,384]{2,1,0:T(8,128)(2,1)S(1)} %copy-done), kind=kOutput, calls=%fused_computation.36 | convolution fusion | flops 454459392 | bytes 3244032 | tf_op jit(solution)/shard_map/ceij,kj->ceik/dot_general | solution.py:39
  78.9 0.6 copy.47
  79.5 12.8 %all_to_all.32 = bf16[2,1,384,384]{3,0,1,2:T(2,128)(2,1)S(1)} all-to-all(bf16[2,1,384,384]{3,0,1,2:T(2,128)(2,1)S(1)} %copy.47), channel_id=1, replica_groups=mesh['energy'=8,'space'=4] {'energy'}, dimensions={2} | all-to-all | bytes 1179648 | tf_op jit(solution)/shard_map/all_to_all | solution.py:81
  92.3 2.9 %slice_reduce_fusion = (bf16[384,384]{1,0:T(8,128)(2,1)S(1)}, bf16[384,384]{1,0:T(8,128)(2,1)S(1)}) fusion(bf16[2,1,384,384]{3,0,1,2:T(2,128)(2,1)S(1)} %all_to_all.32), kind=kLoop, calls=%fused_computation.39 | loop fusion | bytes 1179648 | tf_op jit(solution)/shard_map/slice | solution.py:83
  95.2 0.1 squeeze.35
  95.4 0.1 squeeze.34
  95.5 0.7 fusion.40
  96.2 0.7 fusion.38
  96.9 0.7 convolution_subtract_fusion
  97.6 0.6 copy-done.1
  98.1 1.0 %multiply_add_fusion = (f32[16,18432]{1,0:T(8,128)S(1)}, f32[16,18432]{1,0:T(8,128)S(1)}) fusion(f32[16,18432]{1,0:T(8,128)S(1)} %convolution_subtract_fusion.2, f32[16,18432]{1,0:T(8,128)S(1)} %copy-done.1, f32[16,18432]{1,0:T(8,128)S(1)} %convolution_subtract_fusion, f32[16,18432]{1,0:T(8,128)S(1)} %fusion.38, bf16[8,18432]{1,0:T(8,128)(2,1)S(1)} %squeeze.34, ...), kind=kOutput, calls=%fused_computation.35 | convolution fusion | flops 30377728 | bytes 7372832 | tf_op jit(solution)/shard_map/dot_general | solution.py:15
  99.2 0.7 fusion.36
  99.9 0.7 fusion.34
  100.7 0.8 fusion.10
  101.5 0.7 fusion.11
  102.3 0.9 pad_maximum_fusion.1
  (8 shorter events, 0.2 us)
Async XLA Ops:
  0.0 54.6 %copy-start = (bf16[1,384,384]{2,1,0:T(8,128)(2,1)S(1)}, bf16[1,384,384]{2,1,0:T(8,128)(2,1)}, u32[]{:S(2)}) copy-start(bf16[1,384,384]{2,1,0:T(8,128)(2,1)} %param.6) | copy-start | bytes 884740
  30.0 0.7 copy-start.3
  54.6 6.6 %copy-start.2 = (bf16[1,384,384]{2,1,0:T(8,128)(2,1)S(1)}, bf16[1,384,384]{2,1,0:T(8,128)(2,1)}, u32[]{:S(2)}) copy-start(bf16[1,384,384]{2,1,0:T(8,128)(2,1)} %param.5) | copy-start | bytes 884740
  56.5 15.2 %collective-permute-start.1 = (bf16[2,1,384,384]{3,2,0,1:T(8,128)(2,1)}, bf16[2,1,384,384]{3,2,0,1:T(8,128)(2,1)}, u32[]{:S(2)}, u32[]{:S(2)}) collective-permute-start(bf16[2,1,384,384]{3,2,0,1:T(8,128)(2,1)} %fusion.17), channel_id=1, source_target_pairs={{1,0},{2,1},{3,2},{5,4},{6,5},{7,6},{9,8},{10,9},{11,10},{13,12},{... | collective-permute-start | bytes 1769480 | tf_op jit(solution)/shard_map/ppermute | solution.py:11
  59.7 16.9 %collective-permute-start = (bf16[2,1,384,384]{2,3,0,1:T(8,128)(2,1)}, bf16[2,1,384,384]{2,3,0,1:T(8,128)(2,1)}, u32[]{:S(2)}, u32[]{:S(2)}) collective-permute-start(bf16[2,1,384,384]{2,3,0,1:T(8,128)(2,1)} %copy.43), channel_id=1, source_target_pairs={{0,1},{1,2},{2,3},{4,5},{5,6},{6,7},{8,9},{9,10},{10,11},{12,13},{... | collective-permute-start | bytes 1769480 | tf_op jit(solution)/shard_map/ppermute | solution.py:11
  96.9 1.3 %copy-start.1 = (f32[16,18432]{1,0:T(8,128)S(1)}, f32[16,18432]{1,0:T(8,128)}, u32[]{:S(2)}) copy-start(f32[16,18432]{1,0:T(8,128)} %get-tuple-element.15) | copy-start | bytes 3538948
where the time goes:
time: 104 us; the launch traced here: 103 us
  blocking collectives  45.9 us (44%)
  matrix products  20.9 us (20%)
  local copies, waits for them, and re-layouts  16.1 us (15%)
  waiting for transfers between devices  14.3 us (14%)
  starting transfers between devices  4.7 us (5%)
    all_to_all x1, blocking collectives, shards(): lax.all_to_all(green[:, :, 0], 'energy', split_axis=2, concat_axis=1, til...  20.3 us
    dot_general x20, matrix products, apply_table(): jnp.dot(table, values, precision=lax.Precision.HIGHEST, preferred_element...  15.7 us
    ppermute x2, waiting for transfers between devices, shifted(): lax.ppermute(value, axis, [(source, source + steps) for source in range(l...  14.3 us
    all_to_all x1, blocking collectives, shards(): lax.all_to_all(polar_slot, 'energy', split_axis=1, concat_axis=2, tiled=T...  12.8 us
    all_to_all x1, blocking collectives, shards(): lax.all_to_all(screened, 'energy', split_axis=2, concat_axis=1, tiled=True)  12.8 us
    slice x1, local copies, waits for them, and re-layouts, shards(): flattened[2]  7.53 us
    ppermute x2, starting transfers between devices, shifted(): lax.ppermute(value, axis, [(source, source + steps) for source in range(l...  4.7 us
    dot_general x2, matrix products, sandwich(): jnp.einsum('ceij,kj->ceik', left, matrix, preferred_element_type=jnp.floa...  3.35 us
  transfers between devices with their start and end apart: 2, of which 2 were waited for; matrix products, arithmetic and copies ran while one was open for 1% of the time, Pallas kernels for 0%

commit v1 on v0

--- a/solution.py
+++ b/solution.py
@@ -55,7 +55,12 @@
     cos_table = jnp.cos(angles)
     sin_table = jnp.sin(angles)
     scaling = energies ** (-0.5)
-    arrived = lax.all_to_all(green[:, :, 0], "energy", split_axis=2, concat_axis=1, tiled=True)
+    arrived = jnp.concatenate(
+        lax.all_to_all(
+            jnp.stack(jnp.split(green[:, :, 0], lax.axis_size("energy"), axis=2)), "energy", 0, 0
+        ),
+        axis=1,
+    )
     row_count = arrived.shape[2]
     col_count = arrived.shape[3]
     flattened = arrived.reshape((4, energies, row_count * col_count)).astype(jnp.float32)

time: 104 us -> 98 us (0.942)
  local copies, waits for them, and re-layouts: 16.1 us -> 10.4 us
    slice x1 -> x0, local copies, waits for them, and re-layouts: 7.53 us -> none  [shards(): flattened[2]]
    unnamed x9 -> x22, local copies, waits for them, and re-layouts: 2.88 us -> 5.28 us
where the time goes in v1:
time: 98 us; the launch traced here: 97.6 us
  blocking collectives  45.9 us (47%)
  matrix products  21 us (21%)
  waiting for transfers between devices  14.4 us (15%)
  local copies, waits for them, and re-layouts  10.4 us (11%)
  starting transfers between devices  4.66 us (5%)
    all_to_all x1, blocking collectives, shards(): lax.all_to_all(jnp.stack(jnp.split(green[:, :, 0], lax.axis_size('energy'...  20.3 us
    dot_general x20, matrix products, apply_table(): jnp.dot(table, values, precision=lax.Precision.HIGHEST, preferred_element...  15.7 us
    ppermute x2, waiting for transfers between devices, shifted(): lax.ppermute(value, axis, [(source, source + steps) for source in range(l...  14.4 us
    all_to_all x1, blocking collectives, shards(): lax.all_to_all(polar_slot, 'energy', split_axis=1, concat_axis=2, tiled=T...  12.8 us
    all_to_all x1, blocking collectives, shards(): lax.all_to_all(screened, 'energy', split_axis=2, concat_axis=1, tiled=True)  12.8 us
    unnamed x22, local copies, waits for them, and re-layouts  5.28 us
    ppermute x2, starting transfers between devices, shifted(): lax.ppermute(value, axis, [(source, source + steps) for source in range(l...  4.66 us
    dot_general x2, matrix products, sandwich(): jnp.einsum('ceij,kj->ceik', left, matrix, preferred_element_type=jnp.floa...  3.34 us
  transfers between devices with their start and end apart: 2, of which 2 were waited for; matrix products, arithmetic and copies ran while one was open for 1% of the time, Pallas kernels for 0%

profile of v1, /device:TPU:24, one launch (start us, length us, event | category | flops | bytes accessed | tf_op | source)
XLA Modules:
  0.0 97.6 jit_solution(14082940904769421921)
XLA Ops:
  0.0 1.0 %fusion.33 = bf16[8,4,1,48,384]{4,3,1,2,0:T(8,128)(2,1)S(1)} fusion(bf16[4,1,384,384]{3,2,0,1:T(8,128)(2,1)} %bitcast.149), kind=kLoop, calls=%fused_computation.65 | loop fusion | bytes 294912
  1.0 0.9 fusion.32
  2.0 0.9 fusion.31
  2.9 0.9 fusion.30
  4.0 20.3 %all_to_all.26 = bf16[8,4,1,48,384]{4,3,1,2,0:T(8,128)(2,1)S(1)} all-to-all(bf16[8,4,1,48,384]{4,3,1,2,0:T(8,128)(2,1)S(1)} %fusion.26), channel_id=1, replica_groups=mesh['energy'=8,'space'=4] {'energy'}, dimensions={0} | all-to-all | bytes 2359296 | tf_op jit(solution)/shard_map/all_to_all | solution.py:59
  24.3 0.1 slice_bitcast_fusion.1
  24.4 0.1 copy.55
  24.5 0.1 copy.56
  24.6 0.1 copy.54
  24.7 0.4 copy-done.4
  25.1 0.7 fusion.60
  25.7 0.7 fusion.58
  26.4 0.7 convolution_subtract_fusion.2
  27.1 0.7 fusion.54
  27.7 0.7 fusion.56
  28.4 0.7 convolution_subtract_fusion.1
  29.1 0.7 convolution_add_fusion.1
  29.7 2.1 %multiply_subtract_fusion.1 = (f32[16,18432]{1,0:T(8,128)S(1)}, f32[16,18432]{1,0:T(8,128)S(1)}, f32[16,18432]{1,0:T(8,128)}) fusion(f32[16,18432]{1,0:T(8,128)S(1)} %convolution_subtract_fusion.1, f32[16,18432]{1,0:T(8,128)S(1)} %convolution_subtract_fusion.2, f32[16,18432]{1,0:T(8,128)S(1)} %convolution_add_fusion.1, f32[16,18432]{1,0:T(8,128)S(1)} %fusion.60, ...), kind=kOutput, calls=%fused_computation.37 | convolution fusion | flops 30377728 | bytes 8552480 | tf_op jit(solution)/shard_map/dot_general | solution.py:15
  31.8 0.7 fusion.52
  32.6 0.7 fusion.50
  33.3 0.8 fusion.8
  34.1 0.8 fusion.9
  34.9 0.1 pad_maximum_fusion
  35.0 12.8 %all_to_all.27 = bf16[2,8,48,384]{3,2,0,1:T(8,128)(2,1)S(1)} all-to-all(bf16[2,8,48,384]{3,2,0,1:T(8,128)(2,1)S(1)} %pad_maximum_fusion), channel_id=1, replica_groups=mesh['energy'=8,'space'=4] {'energy'}, dimensions={1} | all-to-all | bytes 1179648 | tf_op jit(solution)/shard_map/all_to_all | solution.py:77
  47.8 0.1 copy.37
  47.9 1.1 %copy.41 = bf16[2,1,384,384]{2,3,0,1:T(8,128)(2,1)} copy(bf16[2,1,384,384]{3,2,0,1:T(8,128)(2,1)S(1)} %bitcast.133) | data formatting | bytes 1179648 | tf_op jit(solution)/shard_map/all_to_all | solution.py:77
  49.0 1.9 %fusion.17 = bf16[2,1,384,384]{3,2,0,1:T(8,128)(2,1)} fusion(bf16[2,384,384]{2,1,0:T(8,128)(2,1)S(1)} %bitcast.134, bf16[1,384,384]{2,1,0:T(8,128)(2,1)S(1)} %copy-done), kind=kOutput, calls=%fused_computation.32 | convolution fusion | flops 453574656 | bytes 1474560 | tf_op jit(solution)/shard_map/ceij,jk->ceik/dot_general | solution.py:46
  50.9 3.2 %collective-permute-start.1 = (bf16[2,1,384,384]{3,2,0,1:T(8,128)(2,1)}, bf16[2,1,384,384]{3,2,0,1:T(8,128)(2,1)}, u32[]{:S(2)}, u32[]{:S(2)}) collective-permute-start(bf16[2,1,384,384]{3,2,0,1:T(8,128)(2,1)} %fusion.17), channel_id=1, source_target_pairs={{1,0},{2,1},{3,2},{5,4},{6,5},{7,6},{9,8},{10,9},{11,10},{13,12},{... | collective-permute-start | bytes 1769480 | tf_op jit(solution)/shard_map/ppermute | solution.py:11
  54.1 1.5 %collective-permute-start = (bf16[2,1,384,384]{2,3,0,1:T(8,128)(2,1)}, bf16[2,1,384,384]{2,3,0,1:T(8,128)(2,1)}, u32[]{:S(2)}, u32[]{:S(2)}) collective-permute-start(bf16[2,1,384,384]{2,3,0,1:T(8,128)(2,1)} %copy.41), channel_id=1, source_target_pairs={{0,1},{1,2},{2,3},{4,5},{5,6},{6,7},{8,9},{9,10},{10,11},{12,13},{... | collective-permute-start | bytes 1769480 | tf_op jit(solution)/shard_map/ppermute | solution.py:11
  55.5 1.1 %fusion.14 = f32[2,384,384]{2,1,0:T(8,128)S(1)} fusion(bf16[2,384,384]{2,1,0:T(8,128)(2,1)S(1)} %bitcast.135, bf16[1,384,384]{2,1,0:T(8,128)(2,1)S(1)} %copy-done.3), kind=kOutput, calls=%fused_computation.29 | convolution fusion | flops 453279744 | bytes 2064384 | tf_op jit(solution)/shard_map/ceij,kj->ceik/dot_general | solution.py:39
  56.6 9.4 %collective-permute-done.1 = bf16[2,1,384,384]{3,2,0,1:T(8,128)(2,1)} collective-permute-done((bf16[2,1,384,384]{3,2,0,1:T(8,128)(2,1)}, bf16[2,1,384,384]{3,2,0,1:T(8,128)(2,1)}, u32[]{:S(2)}, u32[]{:S(2)}) %collective-permute-start.1) | collective-permute-done | bytes 589856 | tf_op jit(solution)/shard_map/ppermute | solution.py:11
  66.0 5.0 %collective-permute-done = bf16[2,1,384,384]{2,3,0,1:T(8,128)(2,1)} collective-permute-done((bf16[2,1,384,384]{2,3,0,1:T(8,128)(2,1)}, bf16[2,1,384,384]{2,3,0,1:T(8,128)(2,1)}, u32[]{:S(2)}, u32[]{:S(2)}) %collective-permute-start) | collective-permute-done | bytes 589856 | tf_op jit(solution)/shard_map/ppermute | solution.py:11
  71.0 2.3 %add_convert_fusion = bf16[2,1,384,384]{3,2,0,1:T(8,128)(2,1)S(1)} fusion(bf16[2,1,384,384]{3,2,0,1:T(8,128)(2,1)} %collective-permute-done.1, f32[2,384,384]{2,1,0:T(8,128)S(1)} %fusion.14, bf16[2,1,384,384]{2,3,0,1:T(8,128)(2,1)} %collective-permute-done, bf16[1,384,384]{2,1,0:T(8,128)(2,1)S(1)} %copy-done), kind=kOutput, calls=%fused_computation.35 | convolution fusion | flops 454459392 | bytes 3244032 | tf_op jit(solution)/shard_map/ceij,kj->ceik/dot_general | solution.py:39
  73.3 0.6 copy.45
  73.9 12.8 %all_to_all.28 = bf16[2,1,384,384]{3,0,1,2:T(2,128)(2,1)S(1)} all-to-all(bf16[2,1,384,384]{3,0,1,2:T(2,128)(2,1)S(1)} %copy.45), channel_id=1, replica_groups=mesh['energy'=8,'space'=4] {'energy'}, dimensions={2} | all-to-all | bytes 1179648 | tf_op jit(solution)/shard_map/all_to_all | solution.py:86
  86.7 2.9 %slice_reduce_fusion = (bf16[384,384]{1,0:T(8,128)(2,1)S(1)}, bf16[384,384]{1,0:T(8,128)(2,1)S(1)}) fusion(bf16[2,1,384,384]{3,0,1,2:T(2,128)(2,1)S(1)} %all_to_all.28), kind=kLoop, calls=%fused_computation.38 | loop fusion | bytes 1179648 | tf_op jit(solution)/shard_map/slice | solution.py:88
  89.6 0.1 squeeze.35
  89.8 0.1 squeeze.34
  89.9 0.7 fusion.48
  90.6 0.7 fusion.46
  91.3 0.7 convolution_subtract_fusion
  92.0 0.6 copy-done.1
  92.5 1.0 %multiply_add_fusion = (f32[16,18432]{1,0:T(8,128)S(1)}, f32[16,18432]{1,0:T(8,128)S(1)}) fusion(f32[16,18432]{1,0:T(8,128)S(1)} %convolution_subtract_fusion.2, f32[16,18432]{1,0:T(8,128)S(1)} %copy-done.1, f32[16,18432]{1,0:T(8,128)S(1)} %convolution_subtract_fusion, f32[16,18432]{1,0:T(8,128)S(1)} %fusion.46, bf16[8,18432]{1,0:T(8,128)(2,1)S(1)} %squeeze.34, ...), kind=kOutput, calls=%fused_computation.34 | convolution fusion | flops 30377728 | bytes 7372832 | tf_op jit(solution)/shard_map/dot_general | solution.py:15
  93.6 0.7 fusion.44
  94.3 0.7 fusion.42
  95.1 0.8 fusion.10
  95.9 0.7 fusion.11
  96.7 0.9 pad_maximum_fusion.1
  (17 shorter events, 0.3 us)
Async XLA Ops:
  0.0 49.0 %copy-start = (bf16[1,384,384]{2,1,0:T(8,128)(2,1)S(1)}, bf16[1,384,384]{2,1,0:T(8,128)(2,1)}, u32[]{:S(2)}) copy-start(bf16[1,384,384]{2,1,0:T(8,128)(2,1)} %param.6) | copy-start | bytes 884740
  0.0 3.9 %copy-start.2 = (bf16[4,1,1,384,384]{4,3,2,1,0:T(8,128)(2,1)S(1)}, bf16[4,1,1,384,384]{4,3,2,1,0:T(8,128)(2,1)}, u32[]{:S(2)}) copy-start(bf16[4,1,1,384,384]{4,3,2,1,0:T(8,128)(2,1)} %param.4) | copy-start | bytes 3538948
  24.4 0.7 copy-start.4
  49.0 6.6 %copy-start.3 = (bf16[1,384,384]{2,1,0:T(8,128)(2,1)S(1)}, bf16[1,384,384]{2,1,0:T(8,128)(2,1)}, u32[]{:S(2)}) copy-start(bf16[1,384,384]{2,1,0:T(8,128)(2,1)} %param.5) | copy-start | bytes 884740
  50.9 15.2 %collective-permute-start.1 = (bf16[2,1,384,384]{3,2,0,1:T(8,128)(2,1)}, bf16[2,1,384,384]{3,2,0,1:T(8,128)(2,1)}, u32[]{:S(2)}, u32[]{:S(2)}) collective-permute-start(bf16[2,1,384,384]{3,2,0,1:T(8,128)(2,1)} %fusion.17), channel_id=1, source_target_pairs={{1,0},{2,1},{3,2},{5,4},{6,5},{7,6},{9,8},{10,9},{11,10},{13,12},{... | collective-permute-start | bytes 1769480 | tf_op jit(solution)/shard_map/ppermute | solution.py:11
  54.1 16.9 %collective-permute-start = (bf16[2,1,384,384]{2,3,0,1:T(8,128)(2,1)}, bf16[2,1,384,384]{2,3,0,1:T(8,128)(2,1)}, u32[]{:S(2)}, u32[]{:S(2)}) collective-permute-start(bf16[2,1,384,384]{2,3,0,1:T(8,128)(2,1)} %copy.41), channel_id=1, source_target_pairs={{0,1},{1,2},{2,3},{4,5},{5,6},{6,7},{8,9},{9,10},{10,11},{12,13},{... | collective-permute-start | bytes 1769480 | tf_op jit(solution)/shard_map/ppermute | solution.py:11
  91.3 1.3 %copy-start.1 = (f32[16,18432]{1,0:T(8,128)S(1)}, f32[16,18432]{1,0:T(8,128)}, u32[]{:S(2)}) copy-start(f32[16,18432]{1,0:T(8,128)} %get-tuple-element.15) | copy-start | bytes 3538948
